TPU v7x, 256 devices: a whole 4x4x8 slice. The times are simulated.
256 devices in a mesh: row: 16 (over z, core), col: 16 (over x, y).
Axes of the slice: x: 4, y: 4, z: 8, core: 2. Of those that a mesh axis runs over, the one named last changes fastest.
Arguments:
- token_ids: int32 [32, 256], P('row'), may hold values from 0 to 16383
- passage_lengths: int32 [32], P('row'), may hold values from 64 to 256, as said below
- embedding: bfloat16 [16384, 4096], P(None, 'col'), may hold values from -8 to 8
- attn_gain: bfloat16 [4096], P('col'), may hold values from 0.25 to 1.75
- final_gain: bfloat16 [4096], P('col'), may hold values from 0.25 to 1.75
- query_weight: bfloat16 [4096, 4096], P('row', 'col'), may hold values from -0.5 to 0.5
- key_weight: bfloat16 [4096, 4096], P('row', 'col'), may hold values from -0.5 to 0.5
- value_weight: bfloat16 [4096, 4096], P('row', 'col'), may hold values from -0.09375 to 0.09375
- out_weight: bfloat16 [4096, 4096], P('row', 'col'), may hold values from -0.09375 to 0.09375
- crosskey_weight: bfloat16 [4096, 4096], P('row', 'col'), may hold values from -0.09375 to 0.09375
- crossvalue_weight: bfloat16 [4096, 4096], P('row', 'col'), may hold values from -0.09375 to 0.09375
Outputs:
- hidden_out: bfloat16 [8192, 4096], P('row', 'col')
- cross_keys: bfloat16 [8192, 16, 256], P('row', 'col')
- cross_values: bfloat16 [8192, 16, 256], P('row', 'col')
Inputs may be any that keep to these rules, and one draw needn't show every extreme that they name: `passage_lengths`: some passage of every draw has all 256 slots valid.
All inputs are finite; a program needn't handle non-finite values.
Results may differ from a plain program's by a relative error of at most 0.0082.
Values may be sent and summed in bfloat16 or wider, within the bound.
No kernel may reach another device: no remote copies, remote signals or barrier semaphores. Data moves between devices by JAX's collectives and lax.ppermute only.
A program may use at most 64 MiB of HBM per device.

v0:
```python
import jax
import jax.numpy as jnp
from jax import lax
from jax.sharding import PartitionSpec as P

D = 4096
HD = 256
PLEN = 256
epsilon = 1e-06
masked_score = -1000000000.0


def scaled_rows(widened, summed, gain_row):
    inverse = lax.rsqrt(summed / D + epsilon)
    return (widened * inverse * gain_row.astype(jnp.float32)).astype(jnp.bfloat16)


def spread_norm(row_block, gain_row, which):
    widened = row_block.astype(jnp.float32)
    partial_sum = jnp.sum(widened * widened, axis=1, keepdims=True)
    if which == 0:
        summed = lax.psum(partial_sum, "col")
        return lax.all_gather(
            scaled_rows(widened, summed, gain_row[None, :]), "col", axis=1, tiled=True
        )
    else:
        summed = lax.psum(partial_sum, "col")
        return lax.all_gather(
            scaled_rows(widened, summed, gain_row[None, :]), "col", axis=1, tiled=True
        )


def add_terms(source, pieces):
    return tuple(
        (
            jnp.dot(source, weight_piece, preferred_element_type=jnp.float32)
            for weight_piece in pieces
        )
    )


def attend(query_rows, key_rows, value_rows, passage_lengths):
    tok_rows, local_width = query_rows.shape
    passages_here = tok_rows // PLEN
    heads_here = local_width // HD
    query_four = query_rows.reshape(passages_here, PLEN, heads_here, HD)
    key_four = key_rows.reshape(passages_here, PLEN, heads_here, HD)
    value_four = value_rows.reshape(passages_here, PLEN, heads_here, HD)
    scores = jnp.einsum(
        "pihd,pjhd->phij", query_four, key_four, preferred_element_type=jnp.float32
    ) * HD ** (-0.5)
    valid = jnp.arange(PLEN, dtype=jnp.int32)[None, :] < passage_lengths[:, None]
    scores = jnp.where(valid[:, None, None, :], scores, masked_score)
    highest = jnp.max(scores, axis=-1, keepdims=True)
    expon = jnp.exp(scores - highest)
    probs = (expon / jnp.sum(expon, axis=-1, keepdims=True)).astype(jnp.bfloat16)
    mixed = jnp.einsum("phij,pjhd->pihd", probs, value_four, preferred_element_type=jnp.float32)
    return mixed.astype(jnp.bfloat16).reshape(tok_rows, local_width)


def shards(
    token_ids,
    passage_lengths,
    embedding,
    attn_gain,
    final_gain,
    query_weight,
    key_weight,
    value_weight,
    out_weight,
    crosskey_weight,
    crossvalue_weight,
):
    embedded = jnp.take(embedding, token_ids.reshape(-1), axis=0)
    normed = spread_norm(embedded, attn_gain, 0)
    tok_rows = normed.shape[0]
    local_width = query_weight.shape[1]
    query_sum, key_sum, value_sum = add_terms(
        normed,
        (
            lax.all_gather(query_weight, "row", axis=0, tiled=True),
            lax.all_gather(key_weight, "row", axis=0, tiled=True),
            lax.all_gather(value_weight, "row", axis=0, tiled=True),
        ),
    )
    attended = attend(
        query_sum.astype(jnp.bfloat16),
        key_sum.astype(jnp.bfloat16),
        value_sum.astype(jnp.bfloat16),
        passage_lengths,
    )
    heads_full = lax.all_gather(attended, "col", axis=1, tiled=True)
    (projected,) = add_terms(heads_full, (lax.all_gather(out_weight, "row", axis=0, tiled=True),))
    hidden_out = (embedded.astype(jnp.float32) + projected).astype(jnp.bfloat16)
    final_normed = spread_norm(hidden_out, final_gain, 1)
    crosskey_sum, crossvalue_sum = add_terms(
        final_normed,
        (
            lax.all_gather(crosskey_weight, "row", axis=0, tiled=True),
            lax.all_gather(crossvalue_weight, "row", axis=0, tiled=True),
        ),
    )
    heads_here = local_width // HD
    cross_keys = crosskey_sum.astype(jnp.bfloat16).reshape(tok_rows, heads_here, HD)
    cross_values = crossvalue_sum.astype(jnp.bfloat16).reshape(tok_rows, heads_here, HD)
    return (hidden_out, cross_keys, cross_values)


def solution(mesh):
    return jax.shard_map(
        shards,
        mesh=mesh,
        in_specs=(
            P("row", None),
            P("row"),
            P(None, "col"),
            P("col"),
            P("col"),
            P("row", "col"),
            P("row", "col"),
            P("row", "col"),
            P("row", "col"),
            P("row", "col"),
            P("row", "col"),
        ),
        out_specs=(P("row", "col"), P("row", "col", None), P("row", "col", None)),
        check_vma=False,
    )
```

profile of v0, /device:TPU:1, one launch (start us, length us, event | category | flops | bytes accessed | tf_op | source)
XLA Modules:
  0.0 447.0 jit_solution(17359749313425114075)
XLA Ops:
  8.6 0.7 copy.22
  9.3 6.0 %gather_fusion = bf16[512,256]{1,0:T(8,128)(2,1)S(1)} fusion(bf16[16384,256]{1,0:T(8,128)(2,1)} %param.13, s32[1024]{0:T(1024)S(1)} %pad_clamp_fusion), kind=kCustom, calls=%fused_computation | custom fusion | bytes 526336 | tf_op jit(solution)/shard_map/jit(_take)/gather | solution.py:74
  15.6 34.2 %psum.14 = f32[512,1]{0,1:T(1,128)S(1)} all-reduce(f32[512,1]{0,1:T(1,128)S(1)} %bitcast.48), channel_id=1, replica_groups=mesh['row'=16,'col'=16] {'col'}, use_global_device_ids=true, to_apply=%region_1.2 | all-reduce | flops 512 | bytes 4096 | tf_op jit(solution)/shard_map/psum | solution.py:22
  49.9 0.8 fusion.12
  52.8 0.7 all-gather.14.cloned.1.call-done
  53.5 58.8 %all-gather.10.cloned.1.call-done = bf16[512,4096]{0,1:T(8,128)(2,1)} async-done(((bf16[512,256]{0,1:T(8,128)(2,1)}), bf16[512,4096]{0,1:T(8,128)(2,1)}) %all-gather.10.cloned.1.call-update) | async-done | bytes 4194320 | tf_op jit(solution)/shard_map/all_gather | solution.py:23
  112.3 4.2 convolution_convert_fusion.4
  116.4 37.4 %all-gather.16.cloned.1.call-done = bf16[4096,256]{1,0:T(8,128)(2,1)} async-done(((bf16[256,256]{1,0:T(8,128)(2,1)}), bf16[4096,256]{1,0:T(8,128)(2,1)}) %all-gather.16.cloned.1.call-update) | async-done | bytes 2097168 | tf_op jit(solution)/shard_map/all_gather | solution.py:82
  153.9 4.2 convolution_convert_fusion.3
  158.7 34.7 %all-gather.12.cloned.1.call-done = bf16[4096,256]{1,0:T(8,128)(2,1)} async-done(((bf16[256,256]{1,0:T(8,128)(2,1)}), bf16[4096,256]{1,0:T(8,128)(2,1)}) %all-gather.12.cloned.1.call-update) | async-done | bytes 2097168 | tf_op jit(solution)/shard_map/all_gather | solution.py:83
  193.4 4.2 convolution_convert_fusion.5
  197.6 1.0 convolution_convert_fusion.2
  198.7 0.7 all-gather.24.cloned.1.call-update
  199.5 33.5 %all-gather.20.cloned.1.call-done = bf16[4096,256]{1,0:T(8,128)(2,1)} async-done(((bf16[256,256]{1,0:T(8,128)(2,1)}), bf16[4096,256]{1,0:T(8,128)(2,1)}) %all-gather.20.cloned.1.call-update) | async-done | bytes 2097168 | tf_op jit(solution)/shard_map/all_gather | solution.py:93
  232.9 61.3 %all-gather.18.cloned.1.call-done = bf16[512,4096]{1,0:T(8,128)(2,1)} async-done(((bf16[512,256]{1,0:T(8,128)(2,1)}), bf16[512,4096]{1,0:T(8,128)(2,1)}) %all-gather.18.cloned.1.call-update) | async-done | bytes 4194320 | tf_op jit(solution)/shard_map/all_gather | solution.py:92
  294.2 4.2 fusion.7
  298.4 31.3 %psum.15 = f32[512,1]{0,1:T(1,128)S(1)} all-reduce(f32[512,1]{0,1:T(1,128)S(1)} %bitcast.54), channel_id=1, replica_groups=mesh['row'=16,'col'=16] {'col'}, use_global_device_ids=true, to_apply=%region_5.6 | all-reduce | flops 512 | bytes 4096 | tf_op jit(solution)/shard_map/psum | solution.py:27
  329.7 0.8 fusion.9
  331.3 0.8 copy.19
  332.1 4.6 %all-gather.24.cloned.1.call-done = bf16[4096,256]{1,0:T(8,128)(2,1)} async-done(((bf16[256,256]{1,0:T(8,128)(2,1)}), bf16[4096,256]{1,0:T(8,128)(2,1)}) %all-gather.24.cloned.1.call-update) | async-done | bytes 2097168 | tf_op jit(solution)/shard_map/all_gather | solution.py:99
  336.7 57.3 %all-gather.22.cloned.1.call-done = bf16[512,4096]{0,1:T(8,128)(2,1)} async-done(((bf16[512,256]{0,1:T(8,128)(2,1)}), bf16[512,4096]{0,1:T(8,128)(2,1)}) %all-gather.22.cloned.1.call-update) | async-done | bytes 4194320 | tf_op jit(solution)/shard_map/all_gather | solution.py:28
  394.0 4.9 %fusion.5 = bf16[512,1,256]{2,0,1:T(8,128)(2,1)} fusion(bf16[512,4096]{0,1:T(8,128)(2,1)} %all-gather.22.cloned.1.call-done, bf16[4096,256]{1,0:T(8,128)(2,1)} %all-gather.24.cloned.1.call-done), kind=kOutput, calls=%fused_computation.14 | convolution fusion | flops 1073872896 | bytes 6553600 | tf_op jit(solution)/shard_map/dot_general | solution.py:36
  398.8 36.7 %all-gather.26.cloned.1.call-done = bf16[4096,256]{1,0:T(8,128)(2,1)} async-done(((bf16[256,256]{1,0:T(8,128)(2,1)}), bf16[4096,256]{1,0:T(8,128)(2,1)}) %all-gather.26.cloned.1.call-update) | async-done | bytes 2097168 | tf_op jit(solution)/shard_map/all_gather | solution.py:100
  435.6 4.9 %fusion.6 = bf16[512,1,256]{2,0,1:T(8,128)(2,1)} fusion(bf16[512,4096]{0,1:T(8,128)(2,1)} %all-gather.22.cloned.1.call-done, bf16[4096,256]{1,0:T(8,128)(2,1)} %all-gather.26.cloned.1.call-done), kind=kOutput, calls=%fused_computation.15 | convolution fusion | flops 1073872896 | bytes 6553600 | tf_op jit(solution)/shard_map/dot_general | solution.py:36
  (36 shorter events, 5.2 us)
Async XLA Ops:
  7.2 8.3 %copy-start = (s32[2,256]{1,0:T(2,128)S(1)}, s32[2,256]{1,0:T(2,128)}, u32[]{:S(2)}) copy-start(s32[2,256]{1,0:T(2,128)} %param.11) | copy-start | bytes 6148
  7.2 46.3 %all-gather.14.cloned.1.call-start = ((), (), s32[]{:S(2)}) async-start(), calls=%async_computation.2 | async-start | bytes 2228224 | tf_op jit(solution)/shard_map/all_gather | solution.py:81
  7.9 104.3 %all-gather.10.cloned.1.call-start = ((), (), s32[]{:S(2)}) async-start(), calls=%async_computation | async-start | bytes 4456448 | tf_op jit(solution)/shard_map/all_gather | solution.py:23
  9.3 43.4 %copy-start.1 = (s32[2]{0:T(128)S(1)}, s32[2]{0:T(128)}, u32[]{:S(2)}) copy-start(s32[2]{0:T(128)} %param.12) | copy-start | bytes 28
  50.7 103.1 %all-gather.16.cloned.1.call-start = ((), (), s32[]{:S(2)}) async-start(), calls=%async_computation.3 | async-start | bytes 2228224 | tf_op jit(solution)/shard_map/all_gather | solution.py:82
  51.5 141.9 %all-gather.12.cloned.1.call-start = ((), (), s32[]{:S(2)}) async-start(), calls=%async_computation.1 | async-start | bytes 2228224 | tf_op jit(solution)/shard_map/all_gather | solution.py:83
  52.0 180.9 %all-gather.20.cloned.1.call-start = ((), (), s32[]{:S(2)}) async-start(), calls=%async_computation.5 | async-start | bytes 2228224 | tf_op jit(solution)/shard_map/all_gather | solution.py:93
  52.6 241.6 %all-gather.18.cloned.1.call-start = ((), (), s32[]{:S(2)}) async-start(), calls=%async_computation.4 | async-start | bytes 4456448 | tf_op jit(solution)/shard_map/all_gather | solution.py:92
  197.6 1.9 copy-start.2
  198.6 138.1 %all-gather.24.cloned.1.call-start = ((), (), s32[]{:S(2)}) async-start(), calls=%async_computation.7 | async-start | bytes 2228224 | tf_op jit(solution)/shard_map/all_gather | solution.py:99
  199.4 194.6 %all-gather.22.cloned.1.call-start = ((), (), s32[]{:S(2)}) async-start(), calls=%async_computation.6 | async-start | bytes 4456448 | tf_op jit(solution)/shard_map/all_gather | solution.py:28
  330.5 105.1 %all-gather.26.cloned.1.call-start = ((), (), s32[]{:S(2)}) async-start(), calls=%async_computation.8 | async-start | bytes 2228224 | tf_op jit(solution)/shard_map/all_gather | solution.py:100
Sparse Core Ops, SparseCore 0:
  9.8 43.6 all-gather.13
  56.5 55.7 all-gather.9
  114.1 39.7 all-gather.15
  155.5 37.8 all-gather.11
  195.1 37.8 all-gather.19
  235.7 58.4 all-gather.17
  296.0 40.6 all-gather.23
  339.7 54.2 all-gather.21
  395.8 39.7 all-gather.25
where the time goes:
time: 447 us
  waiting for transfers between devices  329 us (74%)
  blocking collectives  65.5 us (15%)
  matrix products  28.1 us (6%)
  between operations  14 us (3%)
  local copies, waits for them, and re-layouts  7.71 us (2%)
    all_gather x2, waiting for transfers between devices, spread_norm(): lax.all_gather(scaled_rows(widened, summed, gain_row[None, :]), 'col', ax...  116 us
    psum x2, blocking collectives, spread_norm(): summed = lax.psum(partial_sum, 'col')  65.5 us
    all_gather x1, waiting for transfers between devices, shards(): heads_full = lax.all_gather(attended, 'col', axis=1, tiled=True)  61.3 us
    all_gather x1, waiting for transfers between devices, shards(): lax.all_gather(key_weight, 'row', axis=0, tiled=True)  37.4 us
    all_gather x1, waiting for transfers between devices, shards(): lax.all_gather(crossvalue_weight, 'row', axis=0, tiled=True)  36.7 us
    all_gather x1, waiting for transfers between devices, shards(): lax.all_gather(value_weight, 'row', axis=0, tiled=True)  34.7 us
    all_gather x1, waiting for transfers between devices, shards(): lax.all_gather(out_weight, 'row', axis=0, tiled=True)  33.5 us
    dot_general x6, matrix products, add_terms(): jnp.dot(source, weight_piece, preferred_element_type=jnp.float32)  26.4 us
  transfers between devices with their start and end apart: 9, of which 9 were waited for; matrix products, arithmetic and copies ran while one was open for 7% of the time, Pallas kernels for 0%

commit v1 on v0

--- a/solution.py
+++ b/solution.py
@@ -24,7 +24,9 @@
             scaled_rows(widened, summed, gain_row[None, :]), "col", axis=1, tiled=True
         )
     else:
-        summed = lax.psum(partial_sum, "col")
+        summed = partial_sum
+        for hop in (1, 2, 4, 8):
+            summed = summed + lax.ppermute(summed, "col", [(dev, dev ^ hop) for dev in range(16)])
         return lax.all_gather(
             scaled_rows(widened, summed, gain_row[None, :]), "col", axis=1, tiled=True
         )

time: 447 us -> 447 us (level)
  blocking collectives: 65.5 us -> 34.2 us
  waiting for transfers between devices: 329 us -> 354 us
  starting transfers between devices: 0.35 us -> 6.37 us
    psum x2 -> x1, blocking collectives: 65.5 us -> 34.2 us  [spread_norm(): summed = lax.psum(partial_sum, 'col')]
    all_gather x1, waiting for transfers between devices: 4.6 us -> 23 us  [shards(): lax.all_gather(crosskey_weight, 'row', axis=0, tiled=True)]
    ppermute x0 -> x4, waiting for transfers between devices: none -> 6.99 us  [spread_norm(): lax.ppermute(summed, 'col', [(dev, dev ^ hop) for dev in range(16)])]
    ppermute x0 -> x4, starting transfers between devices: none -> 5.84 us  [spread_norm(): lax.ppermute(summed, 'col', [(dev, dev ^ hop) for dev in range(16)])]
  transfers between devices with their start and end apart: 9 -> 13, of which waited for: 9 -> 13; matrix products, arithmetic and copies ran while one was open for 7% -> 7% of each run, Pallas kernels for 0% -> 0%
where the time goes in v1:
time: 447 us
  waiting for transfers between devices  354 us (79%)
  blocking collectives  34.2 us (8%)
  matrix products  28.1 us (6%)
  between operations  14 us (3%)
  local copies, waits for them, and re-layouts  7.71 us (2%)
  starting transfers between devices  6.37 us (1%)
    all_gather x2, waiting for transfers between devices, spread_norm(): lax.all_gather(scaled_rows(widened, summed, gain_row[None, :]), 'col', ax...  116 us
    all_gather x1, waiting for transfers between devices, shards(): heads_full = lax.all_gather(attended, 'col', axis=1, tiled=True)  61.3 us
    all_gather x1, waiting for transfers between devices, shards(): lax.all_gather(key_weight, 'row', axis=0, tiled=True)  37.4 us
    all_gather x1, waiting for transfers between devices, shards(): lax.all_gather(crossvalue_weight, 'row', axis=0, tiled=True)  36.7 us
    all_gather x1, waiting for transfers between devices, shards(): lax.all_gather(value_weight, 'row', axis=0, tiled=True)  34.7 us
    psum x1, blocking collectives, spread_norm(): summed = lax.psum(partial_sum, 'col')  34.2 us
    all_gather x1, waiting for transfers between devices, shards(): lax.all_gather(out_weight, 'row', axis=0, tiled=True)  33.5 us
    dot_general x6, matrix products, add_terms(): jnp.dot(source, weight_piece, preferred_element_type=jnp.float32)  26.4 us
  transfers between devices with their start and end apart: 13, of which 13 were waited for; matrix products, arithmetic and copies ran while one was open for 7% of the time, Pallas kernels for 0%

profile of v1, /device:TPU:1, one launch (start us, length us, event | category | flops | bytes accessed | tf_op | source)
XLA Modules:
  0.0 447.0 jit_solution(3055371866286816190)
XLA Ops:
  9.3 6.0 %gather_fusion = bf16[512,256]{1,0:T(8,128)(2,1)S(1)} fusion(bf16[16384,256]{1,0:T(8,128)(2,1)} %param.13, s32[1024]{0:T(1024)S(1)} %pad_clamp_fusion), kind=kCustom, calls=%fused_computation | custom fusion | bytes 526336 | tf_op jit(solution)/shard_map/jit(_take)/gather | solution.py:76
  15.6 34.2 %psum.7 = f32[512,1]{0,1:T(1,128)S(1)} all-reduce(f32[512,1]{0,1:T(1,128)S(1)} %bitcast.48), channel_id=1, replica_groups=mesh['row'=16,'col'=16] {'col'}, use_global_device_ids=true, to_apply=%region_1.2 | all-reduce | flops 512 | bytes 4096 | tf_op jit(solution)/shard_map/psum | solution.py:22
  53.5 58.8 %all-gather.10.cloned.1.call-done = bf16[512,4096]{0,1:T(8,128)(2,1)} async-done(((bf16[512,256]{0,1:T(8,128)(2,1)}), bf16[512,4096]{0,1:T(8,128)(2,1)}) %all-gather.10.cloned.1.call-update) | async-done | bytes 4194320 | tf_op jit(solution)/shard_map/all_gather | solution.py:23
  112.3 4.2 convolution_convert_fusion.4
  116.4 37.4 %all-gather.16.cloned.1.call-done = bf16[4096,256]{1,0:T(8,128)(2,1)} async-done(((bf16[256,256]{1,0:T(8,128)(2,1)}), bf16[4096,256]{1,0:T(8,128)(2,1)}) %all-gather.16.cloned.1.call-update) | async-done | bytes 2097168 | tf_op jit(solution)/shard_map/all_gather | solution.py:84
  153.9 4.2 convolution_convert_fusion.3
  158.7 34.7 %all-gather.12.cloned.1.call-done = bf16[4096,256]{1,0:T(8,128)(2,1)} async-done(((bf16[256,256]{1,0:T(8,128)(2,1)}), bf16[4096,256]{1,0:T(8,128)(2,1)}) %all-gather.12.cloned.1.call-update) | async-done | bytes 2097168 | tf_op jit(solution)/shard_map/all_gather | solution.py:85
  193.4 4.2 convolution_convert_fusion.5
  197.6 1.0 convolution_convert_fusion.2
  199.4 33.5 %all-gather.20.cloned.1.call-done = bf16[4096,256]{1,0:T(8,128)(2,1)} async-done(((bf16[256,256]{1,0:T(8,128)(2,1)}), bf16[4096,256]{1,0:T(8,128)(2,1)}) %all-gather.20.cloned.1.call-update) | async-done | bytes 2097168 | tf_op jit(solution)/shard_map/all_gather | solution.py:95
  232.9 61.3 %all-gather.18.cloned.1.call-done = bf16[512,4096]{1,0:T(8,128)(2,1)} async-done(((bf16[512,256]{1,0:T(8,128)(2,1)}), bf16[512,4096]{1,0:T(8,128)(2,1)}) %all-gather.18.cloned.1.call-update) | async-done | bytes 4194320 | tf_op jit(solution)/shard_map/all_gather | solution.py:94
  294.2 4.2 fusion.7
  298.4 1.0 collective-permute-start
  299.4 1.5 collective-permute-done
  300.9 1.8 collective-permute-start.1
  302.8 2.1 collective-permute-done.1
  305.8 1.5 collective-permute-done.2
  307.3 2.1 collective-permute-start.3
  309.4 1.8 collective-permute-done.3
  313.7 23.0 %all-gather.24.cloned.1.call-done = bf16[4096,256]{1,0:T(8,128)(2,1)} async-done(((bf16[256,256]{1,0:T(8,128)(2,1)}), bf16[4096,256]{1,0:T(8,128)(2,1)}) %all-gather.24.cloned.1.call-update) | async-done | bytes 2097168 | tf_op jit(solution)/shard_map/all_gather | solution.py:101
  336.7 57.3 %all-gather.22.cloned.1.call-done = bf16[512,4096]{0,1:T(8,128)(2,1)} async-done(((bf16[512,256]{0,1:T(8,128)(2,1)}), bf16[512,4096]{0,1:T(8,128)(2,1)}) %all-gather.22.cloned.1.call-update) | async-done | bytes 4194320 | tf_op jit(solution)/shard_map/all_gather | solution.py:30
  394.0 4.9 %fusion.5 = bf16[512,1,256]{2,0,1:T(8,128)(2,1)} fusion(bf16[512,4096]{0,1:T(8,128)(2,1)} %all-gather.22.cloned.1.call-done, bf16[4096,256]{1,0:T(8,128)(2,1)} %all-gather.24.cloned.1.call-done), kind=kOutput, calls=%fused_computation.14 | convolution fusion | flops 1073872896 | bytes 6553600 | tf_op jit(solution)/shard_map/dot_general | solution.py:38
  398.9 36.7 %all-gather.26.cloned.1.call-done = bf16[4096,256]{1,0:T(8,128)(2,1)} async-done(((bf16[256,256]{1,0:T(8,128)(2,1)}), bf16[4096,256]{1,0:T(8,128)(2,1)}) %all-gather.26.cloned.1.call-update) | async-done | bytes 2097168 | tf_op jit(solution)/shard_map/all_gather | solution.py:102
  435.6 4.9 %fusion.6 = bf16[512,1,256]{2,0,1:T(8,128)(2,1)} fusion(bf16[512,4096]{0,1:T(8,128)(2,1)} %all-gather.22.cloned.1.call-done, bf16[4096,256]{1,0:T(8,128)(2,1)} %all-gather.26.cloned.1.call-done), kind=kOutput, calls=%fused_computation.15 | convolution fusion | flops 1073872896 | bytes 6553600 | tf_op jit(solution)/shard_map/dot_general | solution.py:38
  (46 shorter events, 10.6 us)
Async XLA Ops:
  7.2 8.3 %copy-start = (s32[2,256]{1,0:T(2,128)S(1)}, s32[2,256]{1,0:T(2,128)}, u32[]{:S(2)}) copy-start(s32[2,256]{1,0:T(2,128)} %param.11) | copy-start | bytes 6148
  7.2 46.3 %all-gather.14.cloned.1.call-start = ((), (), s32[]{:S(2)}) async-start(), calls=%async_computation.2 | async-start | bytes 2228224 | tf_op jit(solution)/shard_map/all_gather | solution.py:83
  7.9 104.3 %all-gather.10.cloned.1.call-start = ((), (), s32[]{:S(2)}) async-start(), calls=%async_computation | async-start | bytes 4456448 | tf_op jit(solution)/shard_map/all_gather | solution.py:23
  9.3 43.4 %copy-start.1 = (s32[2]{0:T(128)S(1)}, s32[2]{0:T(128)}, u32[]{:S(2)}) copy-start(s32[2]{0:T(128)} %param.12) | copy-start | bytes 28
  50.7 103.1 %all-gather.16.cloned.1.call-start = ((), (), s32[]{:S(2)}) async-start(), calls=%async_computation.3 | async-start | bytes 2228224 | tf_op jit(solution)/shard_map/all_gather | solution.py:84
  51.5 141.9 %all-gather.12.cloned.1.call-start = ((), (), s32[]{:S(2)}) async-start(), calls=%async_computation.1 | async-start | bytes 2228224 | tf_op jit(solution)/shard_map/all_gather | solution.py:85
  52.0 180.9 %all-gather.20.cloned.1.call-start = ((), (), s32[]{:S(2)}) async-start(), calls=%async_computation.5 | async-start | bytes 2228224 | tf_op jit(solution)/shard_map/all_gather | solution.py:95
  52.6 241.6 %all-gather.18.cloned.1.call-start = ((), (), s32[]{:S(2)}) async-start(), calls=%async_computation.4 | async-start | bytes 4456448 | tf_op jit(solution)/shard_map/all_gather | solution.py:94
  198.6 138.1 %all-gather.24.cloned.1.call-start = ((), (), s32[]{:S(2)}) async-start(), calls=%async_computation.7 | async-start | bytes 2228224 | tf_op jit(solution)/shard_map/all_gather | solution.py:101
  199.4 110.1 %copy-start.2 = (bf16[256]{0:T(256)(128)(2,1)S(1)}, bf16[256]{0:T(256)(128)(2,1)}, u32[]{:S(2)}) copy-start(bf16[256]{0:T(256)(128)(2,1)} %param.15) | copy-start | bytes 1540
  199.4 194.6 %all-gather.22.cloned.1.call-start = ((), (), s32[]{:S(2)}) async-start(), calls=%async_computation.6 | async-start | bytes 4456448 | tf_op jit(solution)/shard_map/all_gather | solution.py:30
  298.4 2.5 collective-permute-start
  300.9 3.9 collective-permute-start.1
  304.9 2.4 collective-permute-start.2
  307.3 3.9 collective-permute-start.3
  312.1 123.5 %all-gather.26.cloned.1.call-start = ((), (), s32[]{:S(2)}) async-start(), calls=%async_computation.8 | async-start | bytes 2228224 | tf_op jit(solution)/shard_map/all_gather | solution.py:102
Sparse Core Ops, SparseCore 0:
  9.8 43.6 all-gather.13
  56.5 55.7 all-gather.9
  114.1 39.7 all-gather.15
  155.5 37.8 all-gather.11
  195.1 37.8 all-gather.19
  235.7 58.4 all-gather.17
  296.0 40.6 all-gather.23
  339.7 54.2 all-gather.21
  395.9 39.7 all-gather.25
